TPU v7x, 32 devices: a whole 2x2x4 slice. The times are simulated.
32 devices in a mesh: region: 4 (over z), row: 2 (over core), col: 4 (over y, x).
Axes of the slice: x: 2, y: 2, z: 4, core: 2. Of those that a mesh axis runs over, the one named last changes fastest.
Arguments:
- cam_jac: bfloat16 [3, 2, 256, 16384], P(None, None, None, 'region'), may hold values from -1 to 1
- point_rows: bfloat16 [3, 2, 4, 16384], P(None, None, None, 'region'), may hold values from -6 to 6
- track_images: int32 [3, 16384], P(None, 'region'), may hold values from 0 to 3, as said below
- track_counts: int32 [4], replicated, may hold values from 1 to 4096, 8192 in all
Outputs:
- factor: float32 [1024, 1024], P(('region', 'row'), 'col')
- solved: float32 [1024], replicated
Inputs may be any that keep to these rules, and one draw needn't show every extreme that they name: `track_images`: each track's 3 entries are different images of the slab. `track_counts`: entry r counts region r's live tracks, which fill its first slots; later slots hold data that no output reads. The counts sum to 8192, and one region has exactly 4096.
All inputs are finite; a program needn't handle non-finite values.
Results may differ from a plain program's by a relative error of at most 0.0036.
Values may be sent and summed in bfloat16 or wider, within the bound.
A program may use at most 128 MiB of HBM per device.

v0:
```python
import jax
import jax.numpy as jnp
from jax import lax
from jax.sharding import PartitionSpec as P

SLAB_IMAGES = 4
BLOCK = 256
damping = 0.1
point_damping = 0.5


def from_root(value, axis, source):
    kept = jnp.where(lax.axis_index(axis) == source, value, 0).astype(value.dtype)
    return lax.psum(kept, axis)


def lower_solve(factor_parts, first, second, third):
    diag_one, below_one, diag_two, below_far, below_two, diag_three = factor_parts
    out_one = first / diag_one
    out_two = (second - below_one * out_one) / diag_two
    out_three = (third - below_far * out_one - below_two * out_two) / diag_three
    return (out_one, out_two, out_three)


def block_terms(cam, points, selector):
    jac_point = points[:, :, 0:3].astype(jnp.float32)
    errors = points[:, :, 3].astype(jnp.float32)

    def entry(left, right):
        return jnp.sum(jac_point[:, :, left] * jac_point[:, :, right], axis=(0, 1))

    diag_one = jnp.sqrt(entry(0, 0) + point_damping)
    below_one = entry(1, 0) / diag_one
    below_far = entry(2, 0) / diag_one
    diag_two = jnp.sqrt(entry(1, 1) + point_damping - below_one * below_one)
    below_two = (entry(2, 1) - below_far * below_one) / diag_two
    diag_three = jnp.sqrt(
        entry(2, 2) + point_damping - below_far * below_far - below_two * below_two
    )
    factor_parts = (diag_one, below_one, diag_two, below_far, below_two, diag_three)
    coef = jnp.stack(
        lower_solve(factor_parts, jac_point[:, :, 0], jac_point[:, :, 1], jac_point[:, :, 2]),
        axis=0,
    ).astype(jnp.bfloat16)
    grads = [jnp.sum(jac_point[:, :, comp] * errors, axis=(0, 1)) for comp in range(3)]
    point_step = jnp.stack(lower_solve(factor_parts, grads[0], grads[1], grads[2]), axis=0).astype(
        jnp.bfloat16
    )
    coef_wide = coef.astype(jnp.float32)
    products = (
        cam[:, 0, :, None, :].astype(jnp.float32)
        * coef_wide[:, :, 0, :].transpose(1, 0, 2)[:, None, :, :]
    )
    products = (
        products
        + cam[:, 1, :, None, :].astype(jnp.float32)
        * coef_wide[:, :, 1, :].transpose(1, 0, 2)[:, None, :, :]
    )
    schur = selector[0][:, None, None, :] * products[0][None]
    for view in range(1, selector.shape[0]):
        schur = schur + selector[view][:, None, None, :] * products[view][None]
    schur = schur.astype(jnp.bfloat16)
    pick = selector.astype(jnp.bfloat16)
    diagonal = jnp.einsum("krpb,kab->aprb", cam, pick, preferred_element_type=jnp.float32).astype(
        jnp.bfloat16
    )
    err_pick = (errors[None, :, :, :] * selector.transpose(1, 0, 2)[:, :, None, :]).astype(
        jnp.bfloat16
    )
    direct = jnp.einsum("krpb,akrb->ap", cam, err_pick, preferred_element_type=jnp.float32)
    coupled = jnp.einsum("apmb,mb->ap", schur, point_step, preferred_element_type=jnp.float32)
    return (schur, diagonal, direct - coupled)


def panel_factor(column, first_row, end_row):
    chol_block = jnp.linalg.cholesky(column[first_row:end_row])
    parts = [jnp.zeros((first_row, column.shape[1]), column.dtype), chol_block]
    if end_row < column.shape[0]:
        parts.append(
            lax.linalg.triangular_solve(
                chol_block, column[end_row:], left_side=False, lower=True, transpose_a=True
            )
        )
    return jnp.concatenate(parts, axis=0)


def on_device(cam_jac, point_rows, track_images, track_counts):
    regions = lax.axis_size("region")
    row_count = lax.axis_size("row")
    region_at = lax.axis_index("region")
    row_at = lax.axis_index("row")
    col_at = lax.axis_index("col")
    params = cam_jac.shape[2]
    slots = cam_jac.shape[3]
    total_cols = SLAB_IMAGES * params
    row_block = total_cols // (regions * row_count)
    images = track_images.astype(jnp.float32)
    live = (jnp.arange(slots, dtype=jnp.int32) < track_counts[region_at]).astype(jnp.float32)
    depth = live.shape[0]
    tile_rows = regions * row_block
    share = params // row_count
    contract = (((1,), (1,)), ((), ()))

    def block_step(block, carry):
        tile_acc, grad_acc = carry
        start = block * BLOCK
        cam = lax.dynamic_slice_in_dim(cam_jac, start, BLOCK, 3)
        pts = lax.dynamic_slice_in_dim(point_rows, start, BLOCK, 3)
        block_images = lax.dynamic_slice_in_dim(images, start, BLOCK, 1)
        alive = lax.dynamic_slice_in_dim(live, start, BLOCK, 0)
        selector = (
            block_images[:, None, :] == jnp.arange(SLAB_IMAGES, dtype=jnp.float32)[None, :, None]
        ).astype(jnp.float32) * alive[None, None, :]
        schur, diagonal, grad = block_terms(cam, pts, selector)
        schur_grid = schur.reshape(regions, row_count, row_block, 3 * BLOCK)
        row_part = lax.dynamic_index_in_dim(schur_grid, row_at, 1, keepdims=False).reshape(
            tile_rows, 3 * BLOCK
        )
        col_part = lax.dynamic_index_in_dim(schur, col_at, 0, keepdims=False).reshape(
            params, 3 * BLOCK
        )
        tile_acc = tile_acc - lax.dot_general(
            row_part, col_part, contract, preferred_element_type=jnp.float32
        )
        diag_grid = diagonal.reshape(regions, row_count, row_block, 2 * BLOCK)
        diag_rows = lax.dynamic_index_in_dim(diag_grid, row_at, 1, keepdims=False).reshape(
            tile_rows, 2 * BLOCK
        )
        diag_rows = lax.dynamic_slice_in_dim(diag_rows, col_at * share, share, 0)
        diag_col = lax.dynamic_index_in_dim(diagonal, col_at, 0, keepdims=False).reshape(
            params, 2 * BLOCK
        )
        update = lax.dot_general(diag_rows, diag_col, contract, preferred_element_type=jnp.float32)
        current = lax.dynamic_slice_in_dim(tile_acc, col_at * share, share, 0)
        tile_acc = lax.dynamic_update_slice_in_dim(tile_acc, current + update, col_at * share, 0)
        grad_acc = grad_acc + lax.dynamic_index_in_dim(grad, col_at, 0, keepdims=False)
        return (tile_acc, grad_acc)

    start_state = (jnp.zeros((tile_rows, params), jnp.float32), jnp.zeros((params,), jnp.float32))
    tile_acc, grad_acc = lax.fori_loop(0, depth // BLOCK, block_step, start_state)
    held, grad_piece = (
        lax.psum_scatter(tile_acc, "region", scatter_dimension=0, tiled=True),
        lax.psum_scatter(
            grad_acc.reshape(regions, params // regions), "region", scatter_dimension=0, tiled=True
        ),
    )
    gathered = lax.all_gather(grad_piece, ("region", "col"), axis=0, tiled=True)
    gradient = (
        gathered.reshape(regions, SLAB_IMAGES, params // regions)
        .transpose(1, 0, 2)
        .reshape(total_cols)
    )
    row_start = (region_at * row_count + row_at) * row_block
    global_rows = row_start + jnp.arange(row_block, dtype=jnp.int32)
    global_cols = col_at * params + jnp.arange(params, dtype=jnp.int32)
    held = held + damping * (global_rows[:, None] == global_cols[None, :]).astype(jnp.float32)
    factor_mine = jnp.zeros((row_block, params), jnp.float32)
    pieces = []
    for panel in range(SLAB_IMAGES):
        first_row = panel * params
        end_row = first_row + params
        column = lax.all_gather(held, ("region", "row"), axis=0, tiled=True)
        factored = lax.cond(
            col_at == panel,
            lambda whole: panel_factor(whole, first_row, end_row),
            lambda whole: jnp.zeros_like(whole),
            column,
        )
        factored = from_root(factored, "col", panel)
        mine = lax.dynamic_slice_in_dim(factored, row_start, row_block, 0)
        partner = lax.dynamic_slice_in_dim(factored, col_at * params, params, 0)
        held = held - jnp.dot(mine, partner.T, precision=lax.Precision.HIGHEST)
        factor_mine = jnp.where(col_at == panel, mine, factor_mine)
        part_z = lax.linalg.triangular_solve(
            factored[first_row:end_row],
            gradient[first_row:end_row][:, None],
            left_side=True,
            lower=True,
        )[:, 0]
        pieces.append(part_z)
        below = jnp.concatenate(
            [jnp.zeros((end_row, params), jnp.float32), factored[end_row:]], axis=0
        )
        gradient = gradient - jnp.dot(below, part_z, precision=lax.Precision.HIGHEST)
    return (factor_mine, jnp.concatenate(pieces))


def solution(mesh):
    in_specs = (
        P(None, None, None, "region"),
        P(None, None, None, "region"),
        P(None, "region"),
        P(),
    )
    out_specs = (P(("region", "row"), "col"), P())
    return jax.shard_map(
        on_device, mesh=mesh, in_specs=in_specs, out_specs=out_specs, check_vma=False
    )
```

profile of v0, /device:TPU:0, one launch (start us, length us, event | category | flops | bytes accessed | tf_op | source)
XLA Modules:
  0.0 1097.6 jit_solution(16919428303074503304)
XLA Ops:
  11.4 459.7 %while.32 = (s32[]{:T(128)}, f32[512,256]{1,0:T(8,128)}, f32[256]{0:T(256)}, f32[3,4096]{1,0:T(4,128)S(1)}, f32[4096]{0:T(1024)}, /*index=5*/bf16[3,2,256,4096]{...) while((s32[]{:T(128)}, f32[512,256]{1,0:T(8,128)}, ...), condition=%wide.region_10.11_spmd.clone, body=%wide.region_0.10_spmd.clone.sunk | while | flops 252784384 | bytes 64036492 | solution.py:140
  471.3 24.6 %reduce-scatter.2.cloned.1.call-done = f32[128,256]{1,0:T(8,128)} async-done(((f32[512,256]{1,0:T(8,128)}), f32[128,256]{1,0:T(8,128)}) %reduce-scatter.2.cloned.1.call-update) | async-done | bytes 131088 | tf_op jit(solution)/shard_map/reduce_scatter | solution.py:142
  497.6 21.0 %all-gather.6.cloned.1.call-done = f32[1024,256]{1,0:T(8,128)} async-done(((f32[128,256]{1,0:T(8,128)}), f32[1024,256]{1,0:T(8,128)}) %all-gather.6.cloned.1.call-update) | async-done | bytes 1048592 | tf_op jit(solution)/shard_map/all_gather | solution.py:162
  518.6 64.9 %conditional.4 = (f32[1024,256]{1,0:T(8,128)S(1)}) conditional(s32[]{:T(128)} %convert_element_type.162, () %tuple.57, f32[1024,256]{1,0:T(8,128)} %all-gather.6.cloned.1.call-done), branch_computations={%region_12.13_spmd, %region_13.0_spmd} | conditional | flops 504480000 | bytes 15862003 | solution.py:163
  521.4 11.7 %cholesky.214 = f32[128,128]{1,0:T(8,128)S(1)} custom-call(f32[128,128]{1,0:T(8,128)S(1)} %cholesky.346), custom_call_target="Cholesky" | custom-call | tf_op jit(solution)/shard_map/cond/branch_1_fun/jit(cholesky)/cholesky | solution.py:76
  533.1 9.8 custom-call.27
  543.4 11.7 %cholesky.231 = f32[128,128]{1,0:T(8,128)S(1)} custom-call(f32[128,128]{1,0:T(8,128)S(1)} %convolution_subtract_fusion.1), custom_call_target="Cholesky" | custom-call | tf_op jit(solution)/shard_map/cond/branch_1_fun/jit(cholesky)/cholesky | solution.py:76
  557.3 4.0 while.29
  561.3 19.7 %custom-call.16 = f32[2,128,128]{1,2,0:T(8,128)S(1)} custom-call(f32[2,128,128]{2,1,0:T(8,128)S(1)} %get-tuple-element.256), custom_call_target="InvertDiagBlocksLowerTriangular" | custom-call | tf_op jit(solution)/shard_map/cond/branch_1_fun/triangular_solve | solution.py:80
  584.7 50.4 %all-reduce.11.cloned.1.call-done = f32[1024,256]{1,0:T(8,128)} async-done(((f32[1024,256]{1,0:T(8,128)}), f32[1024,256]{1,0:T(8,128)}) %all-reduce.11.cloned.1.call-update) | async-done | bytes 1048592 | tf_op jit(solution)/shard_map/psum | solution.py:14
  637.2 22.3 %all-gather.8.cloned.1.call-done = f32[1024,256]{1,0:T(8,128)} async-done(((f32[128,256]{1,0:T(8,128)}), f32[1024,256]{1,0:T(8,128)}) %all-gather.8.cloned.1.call-update) | async-done | bytes 1048592 | tf_op jit(solution)/shard_map/all_gather | solution.py:162
  659.6 8.2 conditional.5
  669.0 107.6 %all-reduce.13.cloned.1.call-done = f32[1024,256]{1,0:T(8,128)} async-done(((f32[1024,256]{1,0:T(8,128)}), f32[1024,256]{1,0:T(8,128)}) %all-reduce.13.cloned.1.call-update) | async-done | bytes 1048592 | tf_op jit(solution)/shard_map/psum | solution.py:14
  779.4 11.7 %all-reduce.5 = f32[4,64]{1,0:T(4,128)S(1)} all-reduce(f32[4,64]{1,0:T(4,128)S(1)} %reshape.640), channel_id=3, replica_groups=mesh['region'=4,'row'=2,'col'=4] {'region'}, use_global_device_ids=true, to_apply=%region_28.30.clone | all-reduce | flops 256 | bytes 2048
  791.7 37.0 %all-gather = f32[16,1,64]{2,1,0:T(1,128)S(1)} all-gather(f32[1,1,64]{2,1,0:T(1,128)S(1)} %dynamic-slice_bitcast_fusion.1), channel_id=1, replica_groups=mesh['region'=4,'row'=2,'col'=4] {'region','col'}, dimensions={0}, use_global_device_ids=true | all-gather | bytes 4352 | tf_op jit(solution)/shard_map/all_gather | solution.py:147
  828.9 5.6 conditional.6
  839.6 19.7 %custom-call.31 = f32[2,128,128]{1,2,0:T(8,128)S(1)} custom-call(f32[2,128,128]{2,1,0:T(8,128)S(1)} %get-tuple-element.332), custom_call_target="InvertDiagBlocksLowerTriangular" | custom-call | tf_op jit(solution)/shard_map/triangular_solve/custom-call.6 | solution.py:174
  860.7 82.2 %all-reduce.15.cloned.1.call-done = f32[1024,256]{1,0:T(8,128)} async-done(((f32[1024,256]{1,0:T(8,128)}), f32[1024,256]{1,0:T(8,128)}) %all-reduce.15.cloned.1.call-update) | async-done | bytes 1048592 | tf_op jit(solution)/shard_map/psum | solution.py:14
  948.9 19.7 %custom-call.32 = f32[2,128,128]{1,2,0:T(8,128)S(1)} custom-call(f32[2,128,128]{2,1,0:T(8,128)S(1)} %get-tuple-element.333), custom_call_target="InvertDiagBlocksLowerTriangular" | custom-call | tf_op jit(solution)/shard_map/triangular_solve/custom-call.6 | solution.py:174
  970.9 4.8 conditional.7
  976.8 4.0 while.35
  980.8 19.7 %custom-call.33 = f32[2,128,128]{1,2,0:T(8,128)S(1)} custom-call(f32[2,128,128]{2,1,0:T(8,128)S(1)} %get-tuple-element.334), custom_call_target="InvertDiagBlocksLowerTriangular" | custom-call | tf_op jit(solution)/shard_map/triangular_solve/custom-call.6 | solution.py:174
  1001.4 61.7 %all-reduce.17.cloned.1.call-done = f32[1024,256]{1,0:T(8,128)} async-done(((f32[1024,256]{1,0:T(8,128)}), f32[1024,256]{1,0:T(8,128)}) %all-reduce.17.cloned.1.call-update) | async-done | bytes 1048592 | tf_op jit(solution)/shard_map/psum | solution.py:14
  1068.2 19.7 %custom-call.34 = f32[2,128,128]{1,2,0:T(8,128)S(1)} custom-call(f32[2,128,128]{2,1,0:T(8,128)S(1)} %get-tuple-element.335), custom_call_target="InvertDiagBlocksLowerTriangular" | custom-call | tf_op jit(solution)/shard_map/triangular_solve/custom-call.6 | solution.py:174
  (1514 shorter events, 517.5 us)
Async XLA Ops:
  7.2 488.7 %reduce-scatter.2.cloned.1.call-start = ((), (), s32[]{:S(2)}) async-start(), calls=%async_computation.1 | async-start | bytes 655360 | tf_op jit(solution)/shard_map/reduce_scatter | solution.py:142
  11.4 5.8 copy-start.17
  40.1 5.8 copy-start.17
  68.9 5.8 copy-start.17
  97.7 5.8 copy-start.17
  126.4 5.8 copy-start.17
  413.7 5.8 copy-start.17
  471.2 47.4 %all-gather.6.cloned.1.call-start = ((), (), s32[]{:S(2)}) async-start(), calls=%async_computation.2 | async-start | bytes 1179648 | tf_op jit(solution)/shard_map/all_gather | solution.py:162
  497.6 137.5 %all-reduce.11.cloned.1.call-start = ((), (), s32[]{:S(2)}) async-start(), calls=%async_computation.3 | async-start | bytes 2097152 | tf_op jit(solution)/shard_map/psum | solution.py:14
  520.1 60.9 %copy-start.7 = (f32[1024,256]{1,0:T(8,128)S(1)}, f32[1024,256]{1,0:T(8,128)}, u32[]{:S(2)}) copy-start(f32[1024,256]{1,0:T(8,128)} %param.4) | copy-start | bytes 3145732 | tf_op jit(solution)/shard_map/cond
  583.5 51.6 %copy-start.10 = (f32[128,256]{1,0:T(8,128)S(1)}, f32[128,256]{1,0:T(8,128)}, u32[]{:S(2)}) copy-start(f32[128,256]{1,0:T(8,128)} %select_add_fusion.1) | copy-start | bytes 393220
  584.6 75.0 %all-gather.8.cloned.1.call-start = ((), (), s32[]{:S(2)}) async-start(), calls=%async_computation.4 | async-start | bytes 1179648 | tf_op jit(solution)/shard_map/all_gather | solution.py:162
  637.2 139.4 %all-reduce.13.cloned.1.call-start = ((), (), s32[]{:S(2)}) async-start(), calls=%async_computation.5 | async-start | bytes 2097152 | tf_op jit(solution)/shard_map/psum | solution.py:14
  667.8 108.8 %copy-start.9 = (f32[128,256]{1,0:T(8,128)S(1)}, f32[128,256]{1,0:T(8,128)}, u32[]{:S(2)}) copy-start(f32[128,256]{1,0:T(8,128)} %convolution_subtract_fusion.10) | copy-start | bytes 393220
  667.8 110.9 %copy-start.21 = (f32[256]{0:T(256)S(1)}, f32[256]{0:T(256)}, u32[]{:S(2)}) copy-start(f32[256]{0:T(256)} %get-tuple-element.248) | copy-start | bytes 3076
  667.8 111.0 %copy-start.22 = (u32[32]{0:T(128)S(1)}, u32[32]{0:T(128)}, u32[]{:S(2)}) copy-start(u32[32]{0:T(128)} %constant.320) | copy-start | bytes 388
  667.8 161.0 %copy-start.5 = (f32[1024,256]{1,0:T(8,128)S(1)}, f32[1024,256]{1,0:T(8,128)}, u32[]{:S(2)}) copy-start(f32[1024,256]{1,0:T(8,128)} %all-reduce.11.cloned.1.call-done) | copy-start | bytes 3145732
  668.9 160.0 %all-gather.10.cloned.1.call-start = ((), (), s32[]{:S(2)}) async-start(), calls=%async_computation.6 | async-start | bytes 1179648 | tf_op jit(solution)/shard_map/all_gather | solution.py:162
  778.7 164.2 %all-reduce.15.cloned.1.call-start = ((), (), s32[]{:S(2)}) async-start(), calls=%async_computation.7 | async-start | bytes 2097152 | tf_op jit(solution)/shard_map/psum | solution.py:14
  835.6 24.3 %slice-start = ((f32[1024,256]{1,0:T(8,128)}), f32[768,256]{1,0:T(8,128)S(1)}, s32[]{:S(2)}) async-start(f32[1024,256]{1,0:T(8,128)} %all-reduce.11.cloned.1.call-done), calls=%async_computation.10 | async-start | bytes 1572864 | tf_op jit(solution)/shard_map/slice | solution.py:182
  835.6 107.3 %copy-start.8 = (f32[128,256]{1,0:T(8,128)S(1)}, f32[128,256]{1,0:T(8,128)}, u32[]{:S(2)}) copy-start(f32[128,256]{1,0:T(8,128)} %convolution_subtract_fusion.9) | copy-start | bytes 393220
  835.6 109.5 %copy-start.6 = (f32[1024,256]{1,0:T(8,128)S(1)}, f32[1024,256]{1,0:T(8,128)}, u32[]{:S(2)}) copy-start(f32[1024,256]{1,0:T(8,128)} %all-reduce.13.cloned.1.call-done) | copy-start | bytes 3145732
  835.6 135.3 %all-gather.12.cloned.1.call-start = ((), (), s32[]{:S(2)}) async-start(), calls=%async_computation.8 | async-start | bytes 1179648 | tf_op jit(solution)/shard_map/all_gather | solution.py:162
  945.0 118.2 %all-reduce.17.cloned.1.call-start = ((), (), s32[]{:S(2)}) async-start(), calls=%async_computation.9 | async-start | bytes 2097152 | tf_op jit(solution)/shard_map/psum | solution.py:14
  (218 other events, 450.2 us)
Sparse Core Ops, SparseCore 0:
  471.3 24.5 reduce-scatter.1
  498.1 20.4 all-gather.5
  584.7 50.3 all-reduce.10
  637.3 22.2 all-gather.7
  669.1 107.4 all-reduce.12
  778.8 22.0 all-gather.9
  835.7 107.1 all-reduce.14
  945.1 22.4 all-gather.11
  976.9 86.2 all-reduce.16
where the time goes:
time: 1110 us; the launch traced here: 1100 us
  waiting for transfers between devices  370 us (33%)
  local copies, waits for them, and re-layouts  355 us (32%)
  other arithmetic  216 us (19%)
  matrix products  66.7 us (6%)
  blocking collectives  48.6 us (4%)
  loops' own time  27.1 us (2%)
  between operations  14.5 us (1%)
    psum x4, waiting for transfers between devices, from_root(): return lax.psum(kept, axis)  302 us
    another operation x13, other arithmetic, on_device(): lax.linalg.triangular_solve(factored[first_row:end_row], gradient[first_r...  80.8 us
    mul x96, local copies, waits for them, and re-layouts, block_terms(): schur = schur + selector[view][:, None, None, :] * products[view][None]  77.7 us
    mul x80, local copies, waits for them, and re-layouts, block_terms(): schur = selector[0][:, None, None, :] * products[0][None]  61.6 us
    all_gather x4, waiting for transfers between devices, on_device(): column = lax.all_gather(held, ('region', 'row'), axis=0, tiled=True)  43.4 us
    all_gather x1, blocking collectives, on_device(): gathered = lax.all_gather(grad_piece, ('region', 'col'), axis=0, tiled=True)  37 us
    dynamic_slice x32, local copies, waits for them, and re-layouts, block_step(): cam = lax.dynamic_slice_in_dim(cam_jac, start, BLOCK, 3)  35.4 us
    another operation x6, other arithmetic, panel_factor(): chol_block = jnp.linalg.cholesky(column[first_row:end_row])  34 us
  transfers between devices with their start and end apart: 9, of which 7 were waited for; matrix products, arithmetic and copies ran while one was open for 7% of the time, Pallas kernels for 0%

commit v1 on v0

--- a/solution.py
+++ b/solution.py
@@ -11,7 +11,7 @@
 
 def from_root(value, axis, source):
     kept = jnp.where(lax.axis_index(axis) == source, value, 0).astype(value.dtype)
-    return lax.psum(kept, axis)
+    return jnp.sum(lax.all_gather(kept, axis), axis=0)
 
 
 def lower_solve(factor_parts, first, second, third):

time: 1110 us -> 1180 us (1.063)
  blocking collectives: 48.6 us -> 85.5 us
  other arithmetic: 216 us -> 228 us
    psum x4 -> x0, waiting for transfers between devices: 302 us -> none  [from_root(): return lax.psum(kept, axis)]
    all_gather x0 -> x4, waiting for transfers between devices: none -> 267 us  [from_root(): return jnp.sum(lax.all_gather(kept, axis), axis=0)]
    all_gather x4, waiting for transfers between devices: 43.4 us -> 87.9 us  [on_device(): column = lax.all_gather(held, ('region', 'row'), axis=0, tiled=True)]
    all_gather x1, blocking collectives: 37 us -> 75 us  [on_device(): gathered = lax.all_gather(grad_piece, ('region', 'col'), axis=0, tiled=True)]
  transfers between devices with their start and end apart: 9 -> 9, of which waited for: 7 -> 8; matrix products, arithmetic and copies ran while one was open for 7% -> 8% of each run, Pallas kernels for 0% -> 0%
where the time goes in v1:
time: 1180 us; the launch traced here: 1160 us
  waiting for transfers between devices  380 us (32%)
  local copies, waits for them, and re-layouts  357 us (30%)
  other arithmetic  228 us (19%)
  blocking collectives  85.5 us (7%)
  matrix products  71.8 us (6%)
  loops' own time  25.9 us (2%)
  between operations  14.5 us (1%)
    all_gather x4, waiting for transfers between devices, from_root(): return jnp.sum(lax.all_gather(kept, axis), axis=0)  267 us
    all_gather x4, waiting for transfers between devices, on_device(): column = lax.all_gather(held, ('region', 'row'), axis=0, tiled=True)  87.9 us
    another operation x13, other arithmetic, on_device(): lax.linalg.triangular_solve(factored[first_row:end_row], gradient[first_r...  82.3 us
    mul x96, local copies, waits for them, and re-layouts, block_terms(): schur = schur + selector[view][:, None, None, :] * products[view][None]  77.7 us
    all_gather x1, blocking collectives, on_device(): gathered = lax.all_gather(grad_piece, ('region', 'col'), axis=0, tiled=True)  75 us
    mul x80, local copies, waits for them, and re-layouts, block_terms(): schur = selector[0][:, None, None, :] * products[0][None]  61.6 us
    dynamic_slice x32, local copies, waits for them, and re-layouts, block_step(): cam = lax.dynamic_slice_in_dim(cam_jac, start, BLOCK, 3)  35.4 us
    another operation x6, other arithmetic, panel_factor(): chol_block = jnp.linalg.cholesky(column[first_row:end_row])  34 us
  transfers between devices with their start and end apart: 9, of which 8 were waited for; matrix products, arithmetic and copies ran while one was open for 8% of the time, Pallas kernels for 0%

profile of v1, /device:TPU:0, one launch (start us, length us, event | category | flops | bytes accessed | tf_op | source)
XLA Modules:
  0.0 1164.0 jit_solution(16715543250556052876)
XLA Ops:
  11.4 459.1 %while.32 = (s32[]{:T(128)}, f32[512,256]{1,0:T(8,128)}, f32[256]{0:T(256)}, f32[3,4096]{1,0:T(4,128)S(1)}, f32[4096]{0:T(1024)}, /*index=5*/bf16[3,2,256,4096]{...) while((s32[]{:T(128)}, f32[512,256]{1,0:T(8,128)}, ...), condition=%wide.region_10.11_spmd.clone, body=%wide.region_0.10_spmd.clone.sunk | while | flops 252784384 | bytes 64036492 | solution.py:140
  470.6 24.7 %reduce-scatter.2.cloned.1.call-done = f32[128,256]{1,0:T(8,128)} async-done(((f32[512,256]{1,0:T(8,128)}), f32[128,256]{1,0:T(8,128)}) %reduce-scatter.2.cloned.1.call-update) | async-done | bytes 131088 | tf_op jit(solution)/shard_map/reduce_scatter | solution.py:142
  497.0 21.0 %all-gather.14.cloned.1.call-done = f32[1024,256]{1,0:T(8,128)} async-done(((f32[128,256]{1,0:T(8,128)}), f32[1024,256]{1,0:T(8,128)}) %all-gather.14.cloned.1.call-update) | async-done | bytes 1048592 | tf_op jit(solution)/shard_map/all_gather | solution.py:162
  518.0 64.8 %conditional.4 = (f32[1024,256]{1,0:T(8,128)S(1)}) conditional(s32[]{:T(128)} %convert_element_type.162, () %tuple.57, f32[1024,256]{1,0:T(8,128)} %all-gather.14.cloned.1.call-done), branch_computations={%region_12.13_spmd, %region_13.0_spmd} | conditional | flops 504480000 | bytes 15862003 | solution.py:163
  520.7 11.7 %cholesky.214 = f32[128,128]{1,0:T(8,128)S(1)} custom-call(f32[128,128]{1,0:T(8,128)S(1)} %cholesky.346), custom_call_target="Cholesky" | custom-call | tf_op jit(solution)/shard_map/cond/branch_1_fun/jit(cholesky)/cholesky | solution.py:76
  532.5 9.8 custom-call.27
  542.8 11.7 %cholesky.231 = f32[128,128]{1,0:T(8,128)S(1)} custom-call(f32[128,128]{1,0:T(8,128)S(1)} %convolution_subtract_fusion.1), custom_call_target="Cholesky" | custom-call | tf_op jit(solution)/shard_map/cond/branch_1_fun/jit(cholesky)/cholesky | solution.py:76
  560.6 19.7 %custom-call.16 = f32[2,128,128]{1,2,0:T(8,128)S(1)} custom-call(f32[2,128,128]{2,1,0:T(8,128)S(1)} %get-tuple-element.256), custom_call_target="InvertDiagBlocksLowerTriangular" | custom-call | tf_op jit(solution)/shard_map/cond/branch_1_fun/triangular_solve | solution.py:80
  583.9 50.5 %all-gather.22.cloned.1.call-done = f32[4096,256]{1,0:T(8,128)} async-done(((f32[1024,256]{1,0:T(8,128)}), f32[4096,256]{1,0:T(8,128)}) %all-gather.22.cloned.1.call-update) | async-done | bytes 4194320 | tf_op jit(solution)/shard_map/all_gather | solution.py:14
  638.2 22.3 %all-gather.16.cloned.1.call-done = f32[1024,256]{1,0:T(8,128)} async-done(((f32[128,256]{1,0:T(8,128)}), f32[1024,256]{1,0:T(8,128)}) %all-gather.16.cloned.1.call-update) | async-done | bytes 1048592 | tf_op jit(solution)/shard_map/all_gather | solution.py:162
  660.5 8.3 conditional.5
  670.0 107.3 %all-gather.24.cloned.1.call-done = f32[4096,256]{1,0:T(8,128)} async-done(((f32[1024,256]{1,0:T(8,128)}), f32[4096,256]{1,0:T(8,128)}) %all-gather.24.cloned.1.call-update) | async-done | bytes 4194320 | tf_op jit(solution)/shard_map/all_gather | solution.py:14
  781.0 22.3 %all-gather.18.cloned.1.call-done = f32[1024,256]{1,0:T(8,128)} async-done(((f32[128,256]{1,0:T(8,128)}), f32[1024,256]{1,0:T(8,128)}) %all-gather.18.cloned.1.call-update) | async-done | bytes 1048592 | tf_op jit(solution)/shard_map/all_gather | solution.py:162
  803.3 8.8 conditional.6
  813.3 109.6 %all-gather.26.cloned.1.call-done = f32[4096,256]{1,0:T(8,128)} async-done(((f32[1024,256]{1,0:T(8,128)}), f32[4096,256]{1,0:T(8,128)}) %all-gather.26.cloned.1.call-update) | async-done | bytes 4194320 | tf_op jit(solution)/shard_map/all_gather | solution.py:14
  926.7 22.3 %all-gather.20.cloned.1.call-done = f32[1024,256]{1,0:T(8,128)} async-done(((f32[128,256]{1,0:T(8,128)}), f32[1024,256]{1,0:T(8,128)}) %all-gather.20.cloned.1.call-update) | async-done | bytes 1048592 | tf_op jit(solution)/shard_map/all_gather | solution.py:162
  950.9 10.4 all-reduce.5
  962.0 75.0 %all-gather.4 = f32[16,1,64]{2,1,0:T(1,128)S(1)} all-gather(f32[1,1,64]{2,1,0:T(1,128)S(1)} %dynamic-slice_bitcast_fusion.1), channel_id=1, replica_groups=mesh['region'=4,'row'=2,'col'=4] {'region','col'}, dimensions={0}, use_global_device_ids=true | all-gather | bytes 4352 | tf_op jit(solution)/shard_map/all_gather | solution.py:147
  1038.2 4.3 while.33
  1042.6 20.3 %custom-call.31 = f32[2,128,128]{1,2,0:T(8,128)} custom-call(f32[2,128,128]{2,1,0:T(8,128)S(1)} %get-tuple-element.332), custom_call_target="InvertDiagBlocksLowerTriangular" | custom-call | tf_op jit(solution)/shard_map/triangular_solve/custom-call.6 | solution.py:174
  1071.9 20.3 %custom-call.32 = f32[2,128,128]{1,2,0:T(8,128)} custom-call(f32[2,128,128]{2,1,0:T(8,128)S(1)} %get-tuple-element.333), custom_call_target="InvertDiagBlocksLowerTriangular" | custom-call | tf_op jit(solution)/shard_map/triangular_solve/custom-call.6 | solution.py:174
  1096.9 5.3 while.35
  1102.2 20.3 %custom-call.33 = f32[2,128,128]{1,2,0:T(8,128)} custom-call(f32[2,128,128]{2,1,0:T(8,128)S(1)} %get-tuple-element.334), custom_call_target="InvertDiagBlocksLowerTriangular" | custom-call | tf_op jit(solution)/shard_map/triangular_solve/custom-call.6 | solution.py:174
  1136.4 19.7 %custom-call.34 = f32[2,128,128]{1,2,0:T(8,128)S(1)} custom-call(f32[2,128,128]{2,1,0:T(8,128)S(1)} %get-tuple-element.335), custom_call_target="InvertDiagBlocksLowerTriangular" | custom-call | tf_op jit(solution)/shard_map/triangular_solve/custom-call.6 | solution.py:174
  (1521 shorter events, 536.7 us)
Async XLA Ops:
  7.2 488.1 %reduce-scatter.2.cloned.1.call-start = ((), (), s32[]{:S(2)}) async-start(), calls=%async_computation.1 | async-start | bytes 655360 | tf_op jit(solution)/shard_map/reduce_scatter | solution.py:142
  11.4 5.8 copy-start.17
  40.1 5.8 copy-start.17
  68.8 5.8 copy-start.17
  97.5 5.8 copy-start.17
  126.2 5.8 copy-start.17
  154.9 5.8 copy-start.17
  183.6 5.8 copy-start.17
  212.3 5.8 copy-start.17
  327.1 5.8 copy-start.17
  413.1 5.8 copy-start.17
  470.6 47.4 %all-gather.14.cloned.1.call-start = ((), (), s32[]{:S(2)}) async-start(), calls=%async_computation.2 | async-start | bytes 1179648 | tf_op jit(solution)/shard_map/all_gather | solution.py:162
  497.0 137.5 %all-gather.22.cloned.1.call-start = ((), (), s32[]{:S(2)}) async-start(), calls=%async_computation.6 | async-start | bytes 5242880 | tf_op jit(solution)/shard_map/all_gather | solution.py:14
  519.5 60.8 %copy-start.7 = (f32[1024,256]{1,0:T(8,128)S(1)}, f32[1024,256]{1,0:T(8,128)}, u32[]{:S(2)}) copy-start(f32[1024,256]{1,0:T(8,128)} %param.4) | copy-start | bytes 3145732 | tf_op jit(solution)/shard_map/cond
  583.9 76.7 %all-gather.16.cloned.1.call-start = ((), (), s32[]{:S(2)}) async-start(), calls=%async_computation.3 | async-start | bytes 1179648 | tf_op jit(solution)/shard_map/all_gather | solution.py:162
  638.1 139.1 %all-gather.24.cloned.1.call-start = ((), (), s32[]{:S(2)}) async-start(), calls=%async_computation.7 | async-start | bytes 5242880 | tf_op jit(solution)/shard_map/all_gather | solution.py:14
  669.9 133.4 %all-gather.18.cloned.1.call-start = ((), (), s32[]{:S(2)}) async-start(), calls=%async_computation.4 | async-start | bytes 1179648 | tf_op jit(solution)/shard_map/all_gather | solution.py:162
  780.9 142.0 %all-gather.26.cloned.1.call-start = ((), (), s32[]{:S(2)}) async-start(), calls=%async_computation.8 | async-start | bytes 5242880 | tf_op jit(solution)/shard_map/all_gather | solution.py:14
  813.2 135.8 %all-gather.20.cloned.1.call-start = ((), (), s32[]{:S(2)}) async-start(), calls=%async_computation.5 | async-start | bytes 1179648 | tf_op jit(solution)/shard_map/all_gather | solution.py:162
  925.5 23.5 %copy-start.5 = (f32[1024,256]{1,0:T(8,128)}, f32[1024,256]{1,0:T(8,128)S(1)}, u32[]{:S(2)}) copy-start(f32[1024,256]{1,0:T(8,128)S(1)} %reduce_sum.179) | copy-start | bytes 3145732
  926.6 199.5 %all-gather.28.cloned.1.call-start = ((), (), s32[]{:S(2)}) async-start(), calls=%async_computation.9 | async-start | bytes 5242880 | tf_op jit(solution)/shard_map/all_gather | solution.py:14
  1042.6 53.6 %copy-start.6 = (f32[1024,256]{1,0:T(8,128)S(1)}, f32[1024,256]{1,0:T(8,128)}, u32[]{:S(2)}) copy-start(f32[1024,256]{1,0:T(8,128)} %copy-done.5) | copy-start | bytes 3145732
  1071.9 24.2 %copy-start.22 = (s32[2,2]{1,0:T(2,128)}, s32[2,2]{1,0:T(2,128)S(1)}, u32[]{:S(2)}) copy-start(s32[2,2]{1,0:T(2,128)S(1)} %get-tuple-element.1074) | copy-start | bytes 52
  1126.1 6.2 copy-start.23
  (219 other events, 435.9 us)
Sparse Core Ops, SparseCore 0:
  470.7 24.5 reduce-scatter.1
  497.5 20.4 all-gather.13
  584.0 50.4 all-gather.21
  638.3 22.2 all-gather.15
  670.0 107.1 all-gather.23
  781.1 22.2 all-gather.17
  813.3 109.5 all-gather.25
  926.8 22.2 all-gather.19
  950.9 89.4 all-gather.27
